TPU v7x, 256 devices: a whole 4x4x8 slice. The times are simulated.
256 devices in a mesh: band: 64 (over z_lo, x, y, core), sector: 4 (over z_hi).
Axes of the slice: x: 4, y: 4, z: 8 (z_hi: 4, z_lo: 2; z = z_hi * 2 + z_lo), core: 2. Of those that a mesh axis runs over, the one named last changes fastest.
Arguments:
- field: bfloat16 [64, 1440, 72], P('band', 'sector'), may hold values from -6 to 6
- filters: float32 [9, 64, 3, 17], P(None, 'band'), may hold values from -1.2 to 1.2
- reach: int32 [64], P('band'), may hold values from 1 to 8, as said below
- w_enc: bfloat16 [9, 72, 384], replicated, may hold values from -0.25 to 0.25
- gain: float32 [384], replicated, may hold values from 0.5 to 1.5
- w_qkv: bfloat16 [384, 1152], replicated, may hold values from -0.3125 to 0.3125
- w_out: bfloat16 [384, 384], replicated, may hold values from -0.3125 to 0.3125
- tau: float32 [8], replicated, may hold values from 0.25 to 24
- neighbours: int32 [64, 4, 3, 4], P('band', 'sector'), may hold values from 0 to 1, as said below
Outputs:
- output: bfloat16 [64, 1440, 384], P('band', 'sector')
Inputs may be any that keep to these rules, and one draw needn't show every extreme that they name: reach[i] is the filter's longitude reach in row i; it equals 8 in the first and last row. neighbours[b, s, r, t] is 1 where query block (b, s) attends key row b - 1 + r in sector t; it is 1 for the block's own rows in its own sector and 0 for rows outside the grid.
All inputs are finite; a program needn't handle non-finite values.
Results may differ from a plain program's by a relative error of at most 0.03.
Values may be sent and summed in bfloat16 or wider, within the bound.
No kernel may reach another device: no remote copies, remote signals or barrier semaphores. Data moves between devices by JAX's collectives and lax.ppermute only.
A program may use at most 64 MiB of HBM per device.

v0:
```python
import math

import jax
import jax.numpy as jnp
from jax import lax
from jax.sharding import PartitionSpec as P

HEADS = 8
FR = 1
LW = 8
KH = 1


def padded(block, sides, width, periodic):
    for axis, dim in sides:
        count = lax.axis_size(axis)
        forward = [(i, i + 1) for i in range(count - 1)]
        if periodic:
            forward.append((count - 1, 0))
        backward = [(target, source) for source, target in forward]
        low = lax.ppermute(
            lax.slice_in_dim(block, block.shape[dim] - width, None, axis=dim), axis, forward
        )
        high = lax.ppermute(lax.slice_in_dim(block, 0, width, axis=dim), axis, backward)
        block = jnp.concatenate([low, block, high], axis=dim)
    return block


def rotate(values, row_ids, col_ids, nlat, nlon):
    npair = values.shape[-1] // 2
    nhalf = npair // 2
    index = jnp.arange(npair, dtype=jnp.int32)
    lon_freq = jnp.where(index < nhalf, index + 1, 0).astype(jnp.float32)
    lat_freq = jnp.where(index >= nhalf, index - nhalf + 1, 0).astype(jnp.float32)
    lon_angle = 2.0 * math.pi / nlon * col_ids.astype(jnp.float32)
    lat_angle = math.pi / nlat * (row_ids.astype(jnp.float32) + 0.5)
    angle = lat_angle[:, None, None] * lat_freq + lon_angle[None, :, None] * lon_freq
    cosine = jnp.cos(angle)[:, :, None, :]
    sine = jnp.sin(angle)[:, :, None, :]
    first = values[..., :npair]
    second = values[..., npair:]
    return jnp.concatenate([first * cosine - second * sine, first * sine + second * cosine], -1)


def normalize(hidden, gain):
    values = hidden.astype(jnp.float32)
    meansquare = jnp.mean(values * values, -1, keepdims=True)
    return (values * lax.rsqrt(meansquare + 1e-05) * gain).astype(jnp.bfloat16)


def spread(payload):
    cycle_cells = lax.all_gather(payload, "sector", axis=1, tiled=True)
    return padded(cycle_cells, (("band", 0),), KH, False)


def local(field, filters, reach, w_enc, gain, w_qkv, w_out, tau, neighbours):
    rows_dev, lon_dev, channels = field.shape
    d_model = gain.shape[0]
    head_dim = d_model // HEADS
    nlat = rows_dev * lax.axis_size("band")
    nlon = lon_dev * lax.axis_size("sector")
    row_start = lax.axis_index("band") * rows_dev
    col_start = lax.axis_index("sector") * lon_dev
    side_cells = padded(field, (("sector", 1),), LW, True)
    block_cells = padded(side_cells, (("band", 0),), FR, False)
    offsets = jnp.abs(jnp.arange(2 * LW + 1, dtype=jnp.int32) - LW)
    tap_keep = (offsets[None, :] <= reach[:, None]).astype(jnp.float32)
    tap_weights = filters * tap_keep[None, :, None, :]
    shifted = jnp.stack(
        [
            jnp.stack(
                [
                    block_cells[above : above + rows_dev, shift : shift + lon_dev]
                    for shift in range(2 * LW + 1)
                ],
                1,
            )
            for above in range(2 * FR + 1)
        ],
        1,
    )
    conv = jnp.einsum(
        "kiab,iabjc->kijc",
        tap_weights,
        shifted.astype(jnp.float32),
        precision=lax.Precision.HIGHEST,
    ).astype(jnp.bfloat16)
    hidden = jax.nn.gelu(
        jnp.einsum("kijc,kcd->ijd", conv, w_enc, preferred_element_type=jnp.float32)
    ).astype(jnp.bfloat16)
    own_rows = row_start + jnp.arange(rows_dev, dtype=jnp.int32)
    own_cols = col_start + jnp.arange(lon_dev, dtype=jnp.int32)
    normed = normalize(hidden, gain).reshape(rows_dev * lon_dev, d_model)
    proj = jnp.dot(normed, w_qkv, preferred_element_type=jnp.float32)
    proj = proj.reshape(rows_dev, lon_dev, 3, HEADS, head_dim)
    query = rotate(proj[:, :, 0], own_rows, own_cols, nlat, nlon).astype(jnp.bfloat16)
    key_own = rotate(proj[:, :, 1], own_rows, own_cols, nlat, nlon).astype(jnp.bfloat16)
    value_own = proj[:, :, 2].astype(jnp.bfloat16)
    payload = jnp.concatenate(
        [
            key_own.reshape(rows_dev, lon_dev, d_model),
            value_own.reshape(rows_dev, lon_dev, d_model),
        ],
        -1,
    )
    gathered = spread(payload)
    key_rows = gathered.shape[0]
    key_all = gathered[..., :d_model].reshape(key_rows, nlon, HEADS, head_dim)
    value_all = gathered[..., d_model:].reshape(key_rows, nlon, HEADS, head_dim)
    keymask = jnp.repeat(neighbours[0, 0], lon_dev, axis=1).reshape(-1) > 0
    queries = jnp.transpose(query.reshape(rows_dev * lon_dev, HEADS, head_dim), (1, 0, 2))
    key_heads = jnp.transpose(key_all.reshape(key_rows * nlon, HEADS, head_dim), (1, 0, 2))
    value_heads = jnp.transpose(value_all.reshape(key_rows * nlon, HEADS, head_dim), (1, 0, 2))
    inv_root = 1.0 / math.sqrt(head_dim)

    def one_head(operands):
        q_head, k_head, v_head, temper = operands
        scores = jnp.einsum("qd,kd->qk", q_head, k_head, preferred_element_type=jnp.float32)
        scores = scores * (temper * inv_root)
        scores = jnp.where(keymask[None, :], scores, -1e30)
        peak = jnp.max(scores, -1, keepdims=True)
        expo = jnp.exp(scores - peak)
        total = jnp.sum(expo, -1, keepdims=True)
        summed = jnp.dot(expo.astype(jnp.bfloat16), v_head, preferred_element_type=jnp.float32)
        return summed / total

    attended = lax.map(one_head, (queries, key_heads, value_heads, tau))
    attended = (
        jnp.transpose(attended, (1, 0, 2)).reshape(rows_dev * lon_dev, d_model).astype(jnp.bfloat16)
    )
    mixed = jnp.dot(attended, w_out, preferred_element_type=jnp.float32).reshape(
        rows_dev, lon_dev, d_model
    )
    return (hidden.astype(jnp.float32) + mixed).astype(jnp.bfloat16)


def solution(mesh):
    return jax.shard_map(
        local,
        mesh=mesh,
        in_specs=(
            P("band", "sector", None),
            P(None, "band", None, None),
            P("band"),
            P(),
            P(),
            P(),
            P(),
            P(),
            P("band", "sector", None, None),
        ),
        out_specs=P("band", "sector", None),
        check_vma=False,
    )
```

profile of v0, /device:TPU:31, one launch (start us, length us, event | category | flops | bytes accessed | tf_op | source)
XLA Modules:
  0.0 237.7 jit_solution(11369777460939733356)
XLA Ops:
  6.5 0.9 fusion.91
  7.4 3.0 %collective-permute-start = (bf16[1,8,72]{1,2,0:T(8,128)(2,1)S(1)}, bf16[1,8,72]{1,2,0:T(8,128)(2,1)S(1)}, u32[]{:S(2)}, u32[]{:S(2)}) collective-permute-start(bf16[1,8,72]{1,2,0:T(8,128)(2,1)S(1)} %get-tuple-element.317), channel_id=1, source_target_pairs={{0,1},{1,2},{2,3},{3,0},{4,5},{5,6},{6,7},{7,4},{8,9},{9,10},{10,1... | collective-permute-start | bytes 3464 | tf_op jit(solution)/shard_map/ppermute | solution.py:21
  10.4 3.1 %collective-permute-start.1 = (bf16[1,8,72]{1,2,0:T(8,128)(2,1)S(1)}, bf16[1,8,72]{1,2,0:T(8,128)(2,1)S(1)}, u32[]{:S(2)}, u32[]{:S(2)}) collective-permute-start(bf16[1,8,72]{1,2,0:T(8,128)(2,1)S(1)} %get-tuple-element.318), channel_id=1, source_target_pairs={{1,0},{2,1},{3,2},{0,3},{5,4},{6,5},{7,6},{4,7},{9,8},{10,9},{11,1... | collective-permute-start | bytes 3464 | tf_op jit(solution)/shard_map/ppermute | solution.py:24
  14.5 0.7 broadcast_multiply_fusion
  15.2 1.8 copy.1531
  17.0 0.9 pad_maximum_fusion.4
  17.9 3.1 %collective-permute-start.2 = (bf16[1,376,72]{1,2,0:T(8,128)(2,1)S(1)}, bf16[1,376,72]{1,2,0:T(8,128)(2,1)S(1)}, u32[]{:S(2)}, u32[]{:S(2)}) collective-permute-start(bf16[1,376,72]{1,2,0:T(8,128)(2,1)S(1)} %pad_maximum_fusion.4), channel_id=1, source_target_pairs={{0,4},{4,8},{8,12},{12,16},{16,20},{20,24},{24,28},{28,32},{32,36}... | collective-permute-start | bytes 162440 | tf_op jit(solution)/shard_map/ppermute | solution.py:21
  21.0 1.9 collective-permute-start.3
  22.9 0.9 constant_dynamic-update-slice_fusion.33
  23.8 0.9 constant_dynamic-update-slice_fusion.32
  24.7 0.9 constant_dynamic-update-slice_fusion.31
  25.6 0.9 constant_dynamic-update-slice_fusion.30
  26.6 0.9 constant_dynamic-update-slice_fusion.29
  27.5 0.9 constant_dynamic-update-slice_fusion.28
  28.4 0.9 constant_dynamic-update-slice_fusion.27
  29.3 0.9 constant_dynamic-update-slice_fusion.26
  30.2 0.8 constant_dynamic-update-slice_fusion.25
  31.1 0.9 constant_dynamic-update-slice_fusion.24
  36.4 2.3 fusion.30
  38.8 0.7 fusion.41
  39.5 0.8 convolution_bitcast_fusion
  40.4 0.8 subtract_convert_fusion
  41.4 1.1 copy.1532
  42.5 52.8 %all-gather.2.cloned.1.call-done = bf16[1,1440,768]{2,1,0:T(8,128)(2,1)} async-done(((bf16[1,360,768]{2,1,0:T(8,128)(2,1)}), bf16[1,1440,768]{2,1,0:T(8,128)(2,1)}) %all-gather.2.cloned.1.call-update) | async-done | bytes 2211856 | tf_op jit(solution)/shard_map/all_gather | solution.py:52
  95.3 5.2 %collective-permute-start.4 = (bf16[1,1440,768]{2,1,0:T(8,128)(2,1)}, bf16[1,1440,768]{2,1,0:T(8,128)(2,1)}, u32[]{:S(2)}, u32[]{:S(2)}) collective-permute-start(bf16[1,1440,768]{2,1,0:T(8,128)(2,1)} %all-gather.2.cloned.1.call-done), channel_id=1, source_target_pairs={{0,4},{4,8},{8,12},{12,16},{16,20},{20,24},{24,28},{28,32},{32,36}... | collective-permute-start | bytes 6635528 | tf_op jit(solution)/shard_map/ppermute | solution.py:21
  100.5 2.1 collective-permute-start.5
  102.6 0.9 maximum_bitcast_fusion.6
  103.6 21.4 %collective-permute-done.4 = bf16[1,1440,768]{2,1,0:T(8,128)(2,1)} collective-permute-done((bf16[1,1440,768]{2,1,0:T(8,128)(2,1)}, bf16[1,1440,768]{2,1,0:T(8,128)(2,1)}, u32[]{:S(2)}, u32[]{:S(2)}) %collective-permute-start.4) | collective-permute-done | bytes 2211872 | tf_op jit(solution)/shard_map/ppermute | solution.py:21
  125.0 1.8 constant_dynamic-update-slice_fusion.53
  126.9 6.7 %collective-permute-done.5 = bf16[1,1440,768]{2,1,0:T(8,128)(2,1)} collective-permute-done((bf16[1,1440,768]{2,1,0:T(8,128)(2,1)}, bf16[1,1440,768]{2,1,0:T(8,128)(2,1)}, u32[]{:S(2)}, u32[]{:S(2)}) %collective-permute-start.5) | collective-permute-done | bytes 2211872 | tf_op jit(solution)/shard_map/ppermute | solution.py:24
  133.6 1.8 constant_dynamic-update-slice_fusion.51
  135.4 3.4 %fusion.90 = (bf16[3,1440,384]{2,1,0:T(8,128)(2,1)}, bf16[3,1440,384]{2,1,0:T(8,128)(2,1)}) fusion(bf16[3,1440,768]{2,1,0:T(8,128)(2,1)S(1)} %constant_dynamic-update-slice_fusion.51), kind=kLoop, calls=%fused_computation.220 | loop fusion | bytes 13271040 | tf_op jit(solution)/shard_map/slice | solution.py:109
  138.8 8.6 %copy.1533 = bf16[3,1440,384]{1,0,2:T(4,128)(2,1)} copy(bf16[3,1440,384]{2,1,0:T(8,128)(2,1)} %get-tuple-element.308) | data formatting | bytes 6635520 | tf_op jit(solution)/shard_map/slice | solution.py:108
  147.4 9.8 %reshape_reshape.7 = bf16[4320,8,48]{0,2,1:T(8,128)(2,1)} reshape(bf16[3,1440,384]{1,0,2:T(4,128)(2,1)} %copy.1533) | data formatting | bytes 6635520 | tf_op jit(solution)/shard_map/reshape;reshape | solution.py:112
  157.2 8.6 %copy.1534 = bf16[3,1440,384]{1,0,2:T(4,128)(2,1)} copy(bf16[3,1440,384]{2,1,0:T(8,128)(2,1)} %get-tuple-element.307) | data formatting | bytes 6635520 | tf_op jit(solution)/shard_map/slice | solution.py:109
  165.9 9.9 %reshape_reshape.8 = bf16[4320,8,48]{0,2,1:T(8,128)(2,1)} reshape(bf16[3,1440,384]{1,0,2:T(4,128)(2,1)} %copy.1534) | data formatting | bytes 6635520 | tf_op jit(solution)/shard_map/reshape;reshape | solution.py:113
  175.8 54.0 %while.11 = (s32[]{:T(128)}, bf16[8,360,48]{1,2,0:T(8,128)(2,1)S(1)}, bf16[8,360,48]{1,2,0:T(8,128)(2,1)S(1)}, bf16[8,4320,48]{1,2,0:T(8,128)(2,1)}, f32[8]{0:T(...) while((s32[]{:T(128)}, ...), condition=%wide.region_4.5_spmd.clone, body=%wide.region_1.4_spmd.clone.sunk | while | flops 309501376 | bytes 19683840 | solution.py:127
  175.8 0.6 dynamic_slice.42
  177.2 2.1 fusion.103
  179.3 1.0 fusion.104
  180.3 2.2 fusion.105
  182.5 0.6 dynamic_slice.42
  184.0 2.1 fusion.103
  186.1 1.0 fusion.104
  187.1 2.2 fusion.105
  190.7 2.1 fusion.103
  192.8 1.0 fusion.104
  193.8 2.2 fusion.105
  197.5 2.1 fusion.103
  199.6 1.0 fusion.104
  200.6 2.2 fusion.105
  204.2 2.1 fusion.103
  206.3 1.0 fusion.104
  207.3 2.2 fusion.105
  210.9 2.1 fusion.103
  213.1 1.0 fusion.104
  214.1 2.2 fusion.105
  217.7 2.1 fusion.103
  219.8 1.0 fusion.104
  220.8 2.2 fusion.105
  224.4 2.1 fusion.103
  226.6 1.0 fusion.104
  227.6 2.2 fusion.105
  229.8 1.1 fusion.32
  (102 shorter events, 9.8 us)
Async XLA Ops:
  6.5 32.2 %copy-start = (bf16[9,72,384]{2,1,0:T(8,128)(2,1)S(1)}, bf16[9,72,384]{2,1,0:T(8,128)(2,1)}, u32[]{:S(2)}) copy-start(bf16[9,72,384]{2,1,0:T(8,128)(2,1)} %param.14) | copy-start | bytes 1492996
  6.5 25.4 %copy-start.1 = (bf16[1,360,72]{1,2,0:T(8,128)(2,1)S(1)}, bf16[1,360,72]{1,2,0:T(8,128)(2,1)}, u32[]{:S(2)}) copy-start(bf16[1,360,72]{1,2,0:T(8,128)(2,1)} %param.11) | copy-start | bytes 155524
  6.5 88.7 %all-gather.2.cloned.1.call-start = ((), (), s32[]{:S(2)}) async-start(), calls=%async_computation | async-start | bytes 2764800 | tf_op jit(solution)/shard_map/all_gather | solution.py:52
  7.4 9.5 %collective-permute-start = (bf16[1,8,72]{1,2,0:T(8,128)(2,1)S(1)}, bf16[1,8,72]{1,2,0:T(8,128)(2,1)S(1)}, u32[]{:S(2)}, u32[]{:S(2)}) collective-permute-start(bf16[1,8,72]{1,2,0:T(8,128)(2,1)S(1)} %get-tuple-element.317), channel_id=1, source_target_pairs={{0,1},{1,2},{2,3},{3,0},{4,5},{5,6},{6,7},{7,4},{8,9},{9,10},{10,1... | collective-permute-start | bytes 3464 | tf_op jit(solution)/shard_map/ppermute | solution.py:21
  10.4 6.5 %collective-permute-start.1 = (bf16[1,8,72]{1,2,0:T(8,128)(2,1)S(1)}, bf16[1,8,72]{1,2,0:T(8,128)(2,1)S(1)}, u32[]{:S(2)}, u32[]{:S(2)}) collective-permute-start(bf16[1,8,72]{1,2,0:T(8,128)(2,1)S(1)} %get-tuple-element.318), channel_id=1, source_target_pairs={{1,0},{2,1},{3,2},{0,3},{5,4},{6,5},{7,6},{4,7},{9,8},{10,9},{11,1... | collective-permute-start | bytes 3464 | tf_op jit(solution)/shard_map/ppermute | solution.py:24
  17.9 15.0 %collective-permute-start.2 = (bf16[1,376,72]{1,2,0:T(8,128)(2,1)S(1)}, bf16[1,376,72]{1,2,0:T(8,128)(2,1)S(1)}, u32[]{:S(2)}, u32[]{:S(2)}) collective-permute-start(bf16[1,376,72]{1,2,0:T(8,128)(2,1)S(1)} %pad_maximum_fusion.4), channel_id=1, source_target_pairs={{0,4},{4,8},{8,12},{12,16},{16,20},{20,24},{24,28},{28,32},{32,36}... | collective-permute-start | bytes 162440 | tf_op jit(solution)/shard_map/ppermute | solution.py:21
  21.0 13.7 %collective-permute-start.3 = (bf16[1,376,72]{1,2,0:T(8,128)(2,1)S(1)}, bf16[1,376,72]{1,2,0:T(8,128)(2,1)S(1)}, u32[]{:S(2)}, u32[]{:S(2)}) collective-permute-start(bf16[1,376,72]{1,2,0:T(8,128)(2,1)S(1)} %pad_maximum_fusion.4), channel_id=1, source_target_pairs={{4,0},{8,4},{12,8},{16,12},{20,16},{24,20},{28,24},{32,28},{36,32}... | collective-permute-start | bytes 162440 | tf_op jit(solution)/shard_map/ppermute | solution.py:24
  38.8 0.7 copy-start.5
  40.4 62.2 %copy-start.6 = (s32[1,1,3,4]{3,1,2,0:T(1,128)S(1)}, s32[1,1,3,4]{3,1,2,0:T(1,128)}, u32[]{:S(2)}) copy-start(s32[1,1,3,4]{3,1,2,0:T(1,128)} %param.19) | copy-start | bytes 148
  95.3 31.5 %copy-start.2 = (bf16[1,1440,768]{2,1,0:T(8,128)(2,1)S(1)}, bf16[1,1440,768]{2,1,0:T(8,128)(2,1)}, u32[]{:S(2)}) copy-start(bf16[1,1440,768]{2,1,0:T(8,128)(2,1)} %all-gather.2.cloned.1.call-done) | copy-start | bytes 6635524
  95.3 29.7 %collective-permute-start.4 = (bf16[1,1440,768]{2,1,0:T(8,128)(2,1)}, bf16[1,1440,768]{2,1,0:T(8,128)(2,1)}, u32[]{:S(2)}, u32[]{:S(2)}) collective-permute-start(bf16[1,1440,768]{2,1,0:T(8,128)(2,1)} %all-gather.2.cloned.1.call-done), channel_id=1, source_target_pairs={{0,4},{4,8},{8,12},{12,16},{16,20},{20,24},{24,28},{28,32},{32,36}... | collective-permute-start | bytes 6635528 | tf_op jit(solution)/shard_map/ppermute | solution.py:21
  100.5 33.1 %collective-permute-start.5 = (bf16[1,1440,768]{2,1,0:T(8,128)(2,1)}, bf16[1,1440,768]{2,1,0:T(8,128)(2,1)}, u32[]{:S(2)}, u32[]{:S(2)}) collective-permute-start(bf16[1,1440,768]{2,1,0:T(8,128)(2,1)} %all-gather.2.cloned.1.call-done), channel_id=1, source_target_pairs={{4,0},{8,4},{12,8},{16,12},{20,16},{24,20},{28,24},{32,28},{36,32}... | collective-permute-start | bytes 6635528 | tf_op jit(solution)/shard_map/ppermute | solution.py:24
  165.9 9.9 %copy-start.4 = (bf16[8,360,48]{1,2,0:T(8,128)(2,1)S(1)}, bf16[8,360,48]{1,2,0:T(8,128)(2,1)}, u32[]{:S(2)}) copy-start(bf16[8,360,48]{1,2,0:T(8,128)(2,1)} %custom-call.4) | copy-start | bytes 829444
  165.9 9.9 %copy-start.7 = (f32[8]{0:T(128)S(1)}, f32[8]{0:T(128)}, u32[]{:S(2)}) copy-start(f32[8]{0:T(128)} %param.18) | copy-start | bytes 100
  175.8 54.0 %copy-start.3 = (bf16[384,384]{1,0:T(8,128)(2,1)S(1)}, bf16[384,384]{1,0:T(8,128)(2,1)}, u32[]{:S(2)}) copy-start(bf16[384,384]{1,0:T(8,128)(2,1)} %param.17) | copy-start | bytes 884740
Sparse Core Ops, SparseCore 0:
  42.6 52.6 all-gather.1
where the time goes:
time: 240 us; the launch traced here: 238 us
  waiting for transfers between devices  80.9 us (34%)
  local copies, waits for them, and re-layouts  58.4 us (24%)
  matrix products  39.3 us (16%)
  other arithmetic  20.6 us (9%)
  starting transfers between devices  18.4 us (8%)
  between operations  14.6 us (6%)
  loops' own time  5.43 us (2%)
    all_gather x1, waiting for transfers between devices, spread(): cycle_cells = lax.all_gather(payload, 'sector', axis=1, tiled=True)  52.8 us
    ppermute x3, waiting for transfers between devices, padded(): lax.ppermute(lax.slice_in_dim(block, block.shape[dim] - width, None, axis...  21.4 us
    dot_general x8, matrix products, one_head(): jnp.dot(expo.astype(jnp.bfloat16), v_head, preferred_element_type=jnp.flo...  17.4 us
    dot_general x8, matrix products, one_head(): jnp.einsum('qd,kd->qk', q_head, k_head, preferred_element_type=jnp.float32)  17 us
    slice x2, local copies, waits for them, and re-layouts, local(): value_all = gathered[..., d_model:].reshape(key_rows, nlon, HEADS, head_dim)  12.1 us
    ppermute x3, starting transfers between devices, padded(): lax.ppermute(lax.slice_in_dim(block, block.shape[dim] - width, None, axis...  11.3 us
    another operation x1, local copies, waits for them, and re-layouts, local(): value_all.reshape(key_rows * nlon, HEADS, head_dim)  9.86 us
    another operation x1, local copies, waits for them, and re-layouts, local(): key_all.reshape(key_rows * nlon, HEADS, head_dim)  9.81 us
  transfers between devices with their start and end apart: 7, of which 3 were waited for; matrix products, arithmetic and copies ran while one was open for 7% of the time, Pallas kernels for 0%

commit v1 on v0

v1 whole, which is shorter than its diff:
```python
import functools
import math

import jax
import jax.numpy as jnp
import numpy as np
from jax import lax
from jax.experimental import pallas as pl
from jax.experimental.pallas import tpu as pltpu
from jax.sharding import PartitionSpec as P

BF = jnp.bfloat16
F32 = jnp.float32
HEADS, HD, D, CIN, NK = 8, 48, 384, 72, 9
LON, LANES, NSEC, NROW = 360, 384, 4, 3
WIDE = NSEC * LANES
CP = 80
NEG = -1e30


def rope_tables():
    pair = np.arange(24)
    lane = np.arange(WIDE)
    lon = (lane // LANES) * LON + lane % LANES
    angle = 2.0 * math.pi / 1440 * lon[None, :] * np.where(pair < 12, pair + 1, 0)[:, None]
    lon_tab = np.stack([np.cos(angle), np.sin(angle)]).astype(np.float32)
    offs = np.arange(NROW) - 1
    lat = math.pi / 64 * offs[:, None] * np.where(pair >= 12, pair - 11, 0)[None, :]
    lat_tab = np.stack([np.cos(lat), np.sin(lat)], 1).astype(np.float32)
    lat_tab = np.broadcast_to(lat_tab[..., None], (NROW, 2, 24, 128))
    return lon_tab, np.ascontiguousarray(lat_tab)


def dot(a, b):
    return jnp.dot(a, b, preferred_element_type=F32)


def window_kernel(keep, rm2, rm1, r0, rp1, rp2, wenc, wqkv, wout, lon_tab, lat_tab, out,
                  ff, taps, toep, gath, conv, norm, keys, vals, qs, hid_own, att):
    raw = (rm2, rm1, r0, rp1, rp2)
    lane = lax.broadcasted_iota(jnp.int32, (CP, 128), 1)
    for row in range(5):
        for u in range(NSEC):
            left = raw[row][(u + 3) % 4, :, 256:384].astype(F32)
            right = raw[row][(u + 1) % 4, :, 0:128].astype(F32)
            first = raw[row][u, :, 0:128].astype(F32)
            last = raw[row][u, :, 256:384].astype(F32)
            first = jnp.where(lane < 8, pltpu.roll(left, 24, 1), first)
            turned = pltpu.roll(right, 104, 1)
            last = jnp.where((lane >= 112) & (lane < 120), turned, last)
            ff[row, u, :, 0:128] = first.astype(BF)
            ff[row, u, :, 128:256] = raw[row][u, :, 128:256]
            ff[row, u, :, 256:384] = last.astype(BF)
    for row in range(NROW):
        for k in range(NK):
            block = raw[row + 1][k // 8, 72:80, :].astype(F32)
            for a in range(3):
                taps[row, k * 3 + a : k * 3 + a + 1, :] = block[
                    k % 8 : k % 8 + 1, a * 128 : a * 128 + 128
                ]
    toep[432:512, :] = jnp.zeros((80, NK * 128), BF)
    jp = lax.broadcasted_iota(jnp.int32, (128, 128), 0)
    jj = lax.broadcasted_iota(jnp.int32, (128, 128), 1)
    lon_pair = lax.broadcasted_iota(jnp.int32, (24, 128), 0) < 12
    sub16 = lax.broadcasted_iota(jnp.int32, (16, LANES), 0)
    lane16 = lax.broadcasted_iota(jnp.int32, (16, LANES), 1)

    def rotate(x, c, s):
        x1, x2 = x[0:24], x[24:48]
        return jnp.concatenate([x1 * c - x2 * s, x1 * s + x2 * c], 0)

    def encode(r, carry):
        tp = taps[r]
        for k in range(NK):
            for a in range(3):
                i = k * 3 + a
                base = jnp.broadcast_to(tp[i : i + 1, :], (128, 128))
                circ = pltpu.roll(base, 0, 1, stride=1, stride_axis=0)
                main = jnp.where(jj <= jp, circ, 0.0).astype(BF)
                tail = jnp.where(jj > jp, circ, 0.0)[0:16].astype(BF)
                toep[a * 128 : a * 128 + 128, k * 128 : k * 128 + 128] = main
                toep[384 + a * 16 : 400 + a * 16, k * 128 : k * 128 + 128] = tail
        for u in range(NSEC):
            for t in range(3):
                at = (u * 3 + t) * CP
                for a in range(3):
                    gath[at : at + CP, a * 128 : a * 128 + 128] = ff[
                        r + a, u, :, t * 128 : t * 128 + 128
                    ]
                if t < 2:
                    nxt = [
                        ff[r + a, u, :, t * 128 + 128 : t * 128 + 256].astype(F32) for a in range(3)
                    ]
                    rest = jnp.where(
                        lane < 32, pltpu.roll(nxt[1], 16, 1), pltpu.roll(nxt[2], 32, 1)
                    )
                    rest = jnp.where(lane < 16, nxt[0], rest)
                    gath[at : at + CP, 384:512] = rest.astype(BF)
                else:
                    gath[at : at + CP, 384:512] = jnp.zeros((CP, 128), BF)
        for kk in range(5):
            lo, hi = kk * 256, min(kk * 256 + 256, NK * 128)
            got = dot(gath[...], toep[:, lo:hi]).astype(BF)
            for k in range(2 * kk, min(2 * kk + 2, NK)):
                sub = got[:, (k - 2 * kk) * 128 : (k - 2 * kk) * 128 + 128]
                for t in range(12):
                    conv[k * CP : k * CP + CP, t * 128 : t * 128 + 128] = sub[t * CP : t * CP + CP]

        for n in range(3):
            cols = slice(n * 512, n * 512 + 512)
            pre = dot(wenc[...], conv[:, cols])
            inner = pre * (0.7978845608028654 + 0.035677408136300125 * (pre * pre))
            half = 0.5 * pre
            hid = half + half * jnp.tanh(inner)
            hid = hid.astype(BF).astype(F32)
            scale = lax.rsqrt(jnp.sum(hid * hid, 0, keepdims=True) * (1.0 / D) + 1e-5)
            norm[:, cols] = (hid * scale).astype(BF)
            if n == 0:
                @pl.when(r == 1)
                def _():
                    hid_own[...] = hid[:, 0:LANES]
        lat_c, lat_s = lat_tab[r, 0], lat_tab[r, 1]

        for n in range(3):
            cols = slice(n * 512, n * 512 + 512)
            kv = dot(wqkv[D : 3 * D, :], norm[:, cols])
            cos = jnp.concatenate(
                [jnp.where(lon_pair, lon_tab[0, :, n * 512 + i * 128 : n * 512 + i * 128 + 128], lat_c) for i in range(4)], 1)
            sin = jnp.concatenate(
                [jnp.where(lon_pair, lon_tab[1, :, n * 512 + i * 128 : n * 512 + i * 128 + 128], lat_s) for i in range(4)], 1)
            for h in range(HEADS):
                kh = rotate(kv[h * HD : h * HD + HD], cos, sin)
                keys[r, h, 0:HD, cols] = kh.astype(BF)
                vals[r, h, 0:HD, cols] = kv[D + h * HD : D + h * HD + HD].astype(BF)
        ones = jnp.where(sub16 == 0, 1.0, 0.0).astype(BF)
        for u in range(NSEC):
            ok = jnp.where(keep[r * NSEC + u] > 0, LON, 0)
            bias = jnp.where((sub16 == 0) & (lane16 >= ok), NEG, 0.0).astype(BF)
            for h in range(HEADS):
                keys[r, h, HD:64, u * LANES : u * LANES + LANES] = bias
                vals[r, h, HD:64, u * LANES : u * LANES + LANES] = ones

        @pl.when(r == 1)
        def _():
            qt = dot(wqkv[0:D, :], norm[:, 0:LANES])
            cos = jnp.concatenate(
                [jnp.where(lon_pair, lon_tab[0, :, i * 128 : i * 128 + 128], lat_c) for i in range(3)], 1)
            sin = jnp.concatenate(
                [jnp.where(lon_pair, lon_tab[1, :, i * 128 : i * 128 + 128], lat_s) for i in range(3)], 1)
            unit = jnp.where(sub16 == 0, 1.0, 0.0)
            for h in range(HEADS):
                qh = rotate(qt[h * HD : h * HD + HD], cos, sin)
                qh = jnp.concatenate([qh, unit], 0)
                qs[h] = jnp.transpose(qh)[0:LON].astype(BF)

        return carry

    lax.fori_loop(0, NROW, encode, 0)

    QB = 120

    def attend(h2, carry):
        for b in range(LON // QB):
            pieces = []
            for hh in range(2):
                h = h2 * 2 + hh
                q = qs[h, b * QB : b * QB + QB, :]
                s = [dot(q, keys[r, h]) for r in range(NROW)]
                peak = jnp.max(jnp.maximum(jnp.maximum(s[0], s[1]), s[2]), 1, keepdims=True)
                acc = jnp.zeros((QB, 64), F32)
                for r in range(NROW):
                    w = jnp.exp2(s[r] - peak).astype(BF)
                    acc = acc + lax.dot_general(
                        w, vals[r, h], (((1,), (1,)), ((), ())), preferred_element_type=F32
                    )
                pieces.append(acc / acc[:, HD : HD + 1])
            att[h2, b * QB : b * QB + QB, :] = jnp.concatenate(pieces, 1).astype(BF)
        return carry

    lax.fori_loop(0, HEADS // 2, attend, 0)
    mixed = dot(att[0], wout[0:128, :])
    for i in range(1, 4):
        mixed = mixed + dot(att[i], wout[i * 128 : i * 128 + 128, :])
    hid_nat = jnp.transpose(hid_own[...])[0:LON]
    out[...] = (hid_nat + mixed).astype(BF)


def window_call(keep, rows, wenc, wqkv, wout):
    lon_tab, lat_tab = rope_tables()
    vm = pl.BlockSpec(memory_space=pltpu.VMEM)
    return pl.pallas_call(
        window_kernel,
        out_shape=jax.ShapeDtypeStruct((LON, D), BF),
        in_specs=[pl.BlockSpec(memory_space=pltpu.SMEM)] + [vm] * 10,
        out_specs=vm,
        scratch_shapes=[
            pltpu.VMEM((5, NSEC, CP, LANES), BF),
            pltpu.VMEM((NROW, 32, 128), F32),
            pltpu.VMEM((512, NK * 128), BF),
            pltpu.VMEM((12 * CP, 512), BF),
            pltpu.VMEM((NK * CP, WIDE), BF),
            pltpu.VMEM((D, WIDE), BF),
            pltpu.VMEM((NROW, HEADS, 64, WIDE), BF),
            pltpu.VMEM((NROW, HEADS, 64, WIDE), BF),
            pltpu.VMEM((HEADS, LON, 64), BF),
            pltpu.VMEM((D, LANES), F32),
            pltpu.VMEM((4, LON, 128), BF),
        ],
        compiler_params=pltpu.CompilerParams(vmem_limit_bytes=60 * 1024 * 1024),
        name="window",
    )(keep, *rows, wenc, wqkv, wout, jnp.asarray(lon_tab), jnp.asarray(lat_tab))


def prepare_weights(w_enc, gain, w_qkv, w_out, tau):
    wenc = jnp.pad(jnp.transpose(w_enc, (2, 0, 1)), ((0, 0), (0, 0), (0, CP - CIN))).reshape(D, NK * CP)
    scale = jnp.repeat(tau * (math.log2(math.e) / math.sqrt(HD)), HD)
    cols = jnp.concatenate([scale, jnp.ones((2 * D,), F32)])
    wqkv = (w_qkv.astype(F32) * gain[:, None] * cols[None, :]).astype(BF).T
    wout = jnp.pad(w_out.reshape(HEADS, HD, D), ((0, 0), (0, 64 - HD), (0, 0))).reshape(512, D)
    return wenc, wqkv, wout


def prepare_taps(filters, reach):
    f = filters[:, 0]
    offsets = jnp.abs(jnp.arange(17, dtype=jnp.int32) - 8)
    f = jnp.where(offsets[None, None, :] <= reach[0], f, 0.0)
    base = jnp.concatenate(
        [f[:, :, 0:1], jnp.zeros((NK, 3, 111), F32), f[:, :, :0:-1]], -1
    ).reshape(NK, LANES)
    base = jnp.pad(base, ((0, 32 - NK), (0, 0))).astype(BF)
    return base.reshape(4, 8, LANES)


def prepare_field(field):
    return jnp.pad(field[0].T, ((0, 0), (8, LANES - LON - 8)))


def rel_keep(neighbours, s):
    nb = neighbours[0, 0]
    two = jnp.concatenate([nb, nb], 1)
    return lax.dynamic_slice(two, (0, s), (NROW, NSEC)).reshape(NROW * NSEC)


def local(field, filters, reach, w_enc, gain, w_qkv, w_out, tau, neighbours):
    nb, ns = lax.axis_size("band"), lax.axis_size("sector")
    own = prepare_field(field)
    got = [lax.ppermute(own, "sector", [((i + u) % ns, i) for i in range(ns)]) for u in (1, 2, 3)]
    row = jnp.concatenate([jnp.stack([own] + got), prepare_taps(filters, reach)], 1)

    def shifted(d):
        return lax.ppermute(row, "band", [(i + d, i) for i in range(nb) if 0 <= i + d < nb])

    rows = [shifted(-2), shifted(-1), row, shifted(1), shifted(2)]
    keep = rel_keep(neighbours, lax.axis_index("sector"))
    return window_call(keep, rows, *prepare_weights(w_enc, gain, w_qkv, w_out, tau))[None]


def solution(mesh):
    return jax.shard_map(
        local,
        mesh=mesh,
        in_specs=(
            P("band", "sector", None),
            P(None, "band", None, None),
            P("band"),
            P(),
            P(),
            P(),
            P(),
            P(),
            P("band", "sector", None, None),
        ),
        out_specs=P("band", "sector", None),
        check_vma=False,
    )
```

time: 240 us -> 81 us (0.34)
  the two profiles are of different devices: /device:TPU:31 before, /device:TPU:32 now
where the time goes in v1:
time: 81 us; the launch traced here: 80.6 us
  Pallas kernels  38.6 us (48%)
  starting transfers between devices  23.4 us (29%)
  waiting for transfers between devices  8.55 us (11%)
  local copies, waits for them, and re-layouts  6.48 us (8%)
  other arithmetic  2.75 us (3%)
  between operations  0.84 us (1%)
    pallas_call x1, Pallas kernels, window_call(): pl.pallas_call(window_kernel, out_shape=jax.ShapeDtypeStruct((LON, D), BF...  38.6 us
    ppermute x4, starting transfers between devices, shifted(): lax.ppermute(row, 'band', [(i + d, i) for i in range(nb) if 0 <= i + d <...  14.1 us
    ppermute x3, starting transfers between devices, local(): lax.ppermute(own, 'sector', [((i + u) % ns, i) for i in range(ns)])  9.3 us
    ppermute x4, waiting for transfers between devices, shifted(): lax.ppermute(row, 'band', [(i + d, i) for i in range(nb) if 0 <= i + d <...  8.55 us
    unnamed x22, local copies, waits for them, and re-layouts  2.53 us
  transfers between devices with their start and end apart: 7, of which 2 were waited for; matrix products, arithmetic and copies ran while one was open for 9% of the time, Pallas kernels for 0%

profile of v1, /device:TPU:32, one launch (start us, length us, event | category | flops | bytes accessed | tf_op | source)
XLA Modules:
  0.0 80.6 jit_solution(10300284998684858481)
XLA Ops:
  0.0 0.9 %pad_bitcast_fusion.1 = (bf16[1,72,384]{2,1,0:T(8,128)(2,1)S(1)}, bf16[72,384]{1,0:T(8,128)(2,1)S(1)}) fusion(bf16[72,360]{1,0:T(8,128)(2,1)} %bitcast.34), kind=kLoop, calls=%fused_computation.12 | loop fusion | bytes 162432 | tf_op jit(solution)/shard_map/stack | solution.py:248
  0.9 6.4 %collective-permute-start.1 = (bf16[72,384]{1,0:T(8,128)(2,1)S(1)}, bf16[72,384]{1,0:T(8,128)(2,1)S(1)}, u32[]{:S(2)}, u32[]{:S(2)}) collective-permute-start(bf16[72,384]{1,0:T(8,128)(2,1)S(1)} %get-tuple-element.6), channel_id=1, source_target_pairs={{2,0},{3,1},{0,2},{1,3},{6,4},{7,5},{4,6},{5,7},{10,8},{11,9},{8,1... | collective-permute-start | bytes 165896 | tf_op jit(solution)/shard_map/ppermute | solution.py:247
  7.3 0.6 collective-permute-start
  7.8 2.4 %collective-permute-start.2 = (bf16[72,384]{1,0:T(8,128)(2,1)S(1)}, bf16[72,384]{1,0:T(8,128)(2,1)S(1)}, u32[]{:S(2)}, u32[]{:S(2)}) collective-permute-start(bf16[72,384]{1,0:T(8,128)(2,1)S(1)} %get-tuple-element.6), channel_id=1, source_target_pairs={{3,0},{0,1},{1,2},{2,3},{7,4},{4,5},{5,6},{6,7},{11,8},{8,9},{9,10... | collective-permute-start | bytes 165896 | tf_op jit(solution)/shard_map/ppermute | solution.py:247
  10.9 0.7 broadcast_multiply_fusion
  11.5 0.7 bitcast_select_fusion
  12.3 0.1 slice.10
  12.3 0.1 rev.3
  12.4 0.1 pad.28.clone
  12.5 0.1 pad_maximum_fusion.1
  12.6 0.1 broadcast_in_dim.28
  12.7 0.1 reshape.35
  12.8 0.0 copy-start.7
  12.8 1.8 %copy.14 = bf16[384,1152]{0,1:T(8,128)(2,1)S(1)} copy(bf16[384,1152]{1,0:T(8,128)(2,1)} %param.16) | data formatting | bytes 1769472 | tf_op args[5]
  14.6 0.0 collective-permute-done.1
  14.6 0.0 collective-permute-done
  14.6 0.0 collective-permute-done.2
  14.6 0.0 copy-start
  14.7 0.0 copy-start.8
  14.7 0.0 copy-start.2
  14.7 0.0 copy-start.1
  14.7 7.7 %collective-permute-start.6 = (bf16[4,80,384]{2,1,0:T(8,128)(2,1)S(1)}, bf16[4,80,384]{2,1,0:T(8,128)(2,1)S(1)}, u32[]{:S(2)}, u32[]{:S(2)}) collective-permute-start(bf16[4,80,384]{2,1,0:T(8,128)(2,1)S(1)} %pad_maximum_fusion.r0), channel_id=1, source_target_pairs={{8,0},{12,4},{16,8},{20,12},{24,16},{28,20},{32,24},{36,28},{40,32... | collective-permute-start | bytes 737288 | tf_op jit(solution)/shard_map/ppermute | solution.py:251
  22.4 1.9 %collective-permute-start.5 = (bf16[4,80,384]{2,1,0:T(8,128)(2,1)S(1)}, bf16[4,80,384]{2,1,0:T(8,128)(2,1)S(1)}, u32[]{:S(2)}, u32[]{:S(2)}) collective-permute-start(bf16[4,80,384]{2,1,0:T(8,128)(2,1)S(1)} %pad_maximum_fusion.r0), channel_id=1, source_target_pairs={{4,0},{8,4},{12,8},{16,12},{20,16},{24,20},{28,24},{32,28},{36,32}... | collective-permute-start | bytes 737288 | tf_op jit(solution)/shard_map/ppermute | solution.py:251
  24.3 2.4 %collective-permute-start.4 = (bf16[4,80,384]{2,1,0:T(8,128)(2,1)S(1)}, bf16[4,80,384]{2,1,0:T(8,128)(2,1)S(1)}, u32[]{:S(2)}, u32[]{:S(2)}) collective-permute-start(bf16[4,80,384]{2,1,0:T(8,128)(2,1)S(1)} %pad_maximum_fusion.r0), channel_id=1, source_target_pairs={{0,4},{4,8},{8,12},{12,16},{16,20},{20,24},{24,28},{28,32},{32,36}... | collective-permute-start | bytes 737288 | tf_op jit(solution)/shard_map/ppermute | solution.py:251
  26.7 2.1 %collective-permute-start.3 = (bf16[4,80,384]{2,1,0:T(8,128)(2,1)S(1)}, bf16[4,80,384]{2,1,0:T(8,128)(2,1)S(1)}, u32[]{:S(2)}, u32[]{:S(2)}) collective-permute-start(bf16[4,80,384]{2,1,0:T(8,128)(2,1)S(1)} %pad_maximum_fusion.r0), channel_id=1, source_target_pairs={{0,8},{4,12},{8,16},{12,20},{16,24},{20,28},{24,32},{28,36},{32,40... | collective-permute-start | bytes 737288 | tf_op jit(solution)/shard_map/ppermute | solution.py:251
  28.8 0.0 copy-done.7
  28.9 1.2 %fusion.wqkv = bf16[1152,384]{1,0:T(8,128)(2,1)} fusion(bf16[384,1152]{0,1:T(8,128)(2,1)S(1)} %copy.14, f32[1152]{0:T(1024)S(1)} %concatenate.16, f32[384]{0:T(512)S(1)} %copy-done.7), kind=kLoop, calls=%fused_computation.1 | loop fusion | flops 1769472 | bytes 1775616 | tf_op jit(solution)/shard_map/transpose | solution.py:218
  30.0 0.0 copy-done
  30.0 0.0 copy-done.8
  30.0 0.1 pad_add_fusion
  30.1 0.1 constant_dynamic-slice_fusion
  30.2 0.6 reshape.31.keep
  30.8 0.0 copy-done.2
  30.8 0.8 pad.21
  31.6 0.0 copy-done.1
  31.6 0.1 pad.20
  31.6 1.1 %copy.15.wenc = bf16[384,720]{1,0:T(8,128)(2,1)} copy(bf16[384,720]{0,1:T(8,128)(2,1)S(1)} %bitcast.28) | data formatting | bytes 1105920 | tf_op jit(solution)/shard_map/reshape | solution.py:215
  32.8 0.0 collective-permute-done.6.rp2
  32.8 0.0 copy-start.3
  32.8 0.0 collective-permute-done.5.rp1
  32.8 0.0 copy-start.4
  32.8 3.3 %collective-permute-done.4.rm1 = bf16[4,80,384]{2,1,0:T(8,128)(2,1)S(1)} collective-permute-done((bf16[4,80,384]{2,1,0:T(8,128)(2,1)S(1)}, bf16[4,80,384]{2,1,0:T(8,128)(2,1)S(1)}, u32[]{:S(2)}, u32[]{:S(2)}) %collective-permute-start.4) | collective-permute-done | bytes 245792 | tf_op jit(solution)/shard_map/ppermute | solution.py:251
  36.1 0.0 copy-start.5
  36.1 5.3 %collective-permute-done.3.rm2 = bf16[4,80,384]{2,1,0:T(8,128)(2,1)S(1)} collective-permute-done((bf16[4,80,384]{2,1,0:T(8,128)(2,1)S(1)}, bf16[4,80,384]{2,1,0:T(8,128)(2,1)S(1)}, u32[]{:S(2)}, u32[]{:S(2)}) %collective-permute-start.3) | collective-permute-done | bytes 245792 | tf_op jit(solution)/shard_map/ppermute | solution.py:251
  41.3 0.0 copy-start.6
  41.3 0.0 copy-done.3
  41.3 0.0 copy-done.4
  41.3 0.0 copy-done.5
  41.3 0.7 copy-done.6
  42.0 38.6 %window.1 = bf16[360,384]{1,0:T(8,128)(2,1)} custom-call(s32[12]{0:T(128)} %reshape.31.keep, bf16[4,80,384]{2,1,0:T(8,128)(2,1)} %copy-done.6, bf16[4,80,384]{2,1,0:T(8,128)(2,1)} %copy-done.5, bf16[4,80,384]{2,1,0:T(8,128)(2,1)} %copy-done, bf16[4,80,384]{2,1,0:T(8,128)(2,1)} %copy-done.4, bf16[4,80,384]{2,1,0:T(8,128)(2,1)} %copy-done.3, ...), custom_call_target="tpu_custom_call" | custom-call | tf_op jit(solution)/shard_map/window/pallas_call | solution.py:191
  (8 shorter events, 0.1 us)
Async XLA Ops:
  0.9 13.7 %collective-permute-start.1 = (bf16[72,384]{1,0:T(8,128)(2,1)S(1)}, bf16[72,384]{1,0:T(8,128)(2,1)S(1)}, u32[]{:S(2)}, u32[]{:S(2)}) collective-permute-start(bf16[72,384]{1,0:T(8,128)(2,1)S(1)} %get-tuple-element.6), channel_id=1, source_target_pairs={{2,0},{3,1},{0,2},{1,3},{6,4},{7,5},{4,6},{5,7},{10,8},{11,9},{8,1... | collective-permute-start | bytes 165896 | tf_op jit(solution)/shard_map/ppermute | solution.py:247
  7.3 7.3 %collective-permute-start = (bf16[72,384]{1,0:T(8,128)(2,1)S(1)}, bf16[72,384]{1,0:T(8,128)(2,1)S(1)}, u32[]{:S(2)}, u32[]{:S(2)}) collective-permute-start(bf16[72,384]{1,0:T(8,128)(2,1)S(1)} %get-tuple-element.6), channel_id=1, source_target_pairs={{1,0},{2,1},{3,2},{0,3},{5,4},{6,5},{7,6},{4,7},{9,8},{10,9},{11,1... | collective-permute-start | bytes 165896 | tf_op jit(solution)/shard_map/ppermute | solution.py:247
  7.8 6.8 %collective-permute-start.2 = (bf16[72,384]{1,0:T(8,128)(2,1)S(1)}, bf16[72,384]{1,0:T(8,128)(2,1)S(1)}, u32[]{:S(2)}, u32[]{:S(2)}) collective-permute-start(bf16[72,384]{1,0:T(8,128)(2,1)S(1)} %get-tuple-element.6), channel_id=1, source_target_pairs={{3,0},{0,1},{1,2},{2,3},{7,4},{4,5},{5,6},{6,7},{11,8},{8,9},{9,10... | collective-permute-start | bytes 165896 | tf_op jit(solution)/shard_map/ppermute | solution.py:247
  12.8 16.1 %copy-start.7 = (f32[384]{0:T(512)S(1)}, f32[384]{0:T(512)}, u32[]{:S(2)}) copy-start(f32[384]{0:T(512)} %param.15) | copy-start | bytes 4612
  14.6 15.4 %copy-start = (bf16[4,80,384]{2,1,0:T(8,128)(2,1)}, bf16[4,80,384]{2,1,0:T(8,128)(2,1)S(1)}, u32[]{:S(2)}) copy-start(bf16[4,80,384]{2,1,0:T(8,128)(2,1)S(1)} %pad_maximum_fusion.r0) | copy-start | bytes 737284
  14.7 15.4 %copy-start.8 = (s32[1,1,3,4]{3,1,2,0:T(1,128)S(1)}, s32[1,1,3,4]{3,1,2,0:T(1,128)}, u32[]{:S(2)}) copy-start(s32[1,1,3,4]{3,1,2,0:T(1,128)} %param.19) | copy-start | bytes 148
  14.7 16.1 %copy-start.2 = (bf16[384,384]{1,0:T(8,128)(2,1)S(1)}, bf16[384,384]{1,0:T(8,128)(2,1)}, u32[]{:S(2)}) copy-start(bf16[384,384]{1,0:T(8,128)(2,1)} %param.17) | copy-start | bytes 884740
  14.7 16.9 %copy-start.1 = (bf16[9,72,384]{2,1,0:T(8,128)(2,1)S(1)}, bf16[9,72,384]{2,1,0:T(8,128)(2,1)}, u32[]{:S(2)}) copy-start(bf16[9,72,384]{2,1,0:T(8,128)(2,1)} %param.14) | copy-start | bytes 1492996
  14.7 18.1 %collective-permute-start.6 = (bf16[4,80,384]{2,1,0:T(8,128)(2,1)S(1)}, bf16[4,80,384]{2,1,0:T(8,128)(2,1)S(1)}, u32[]{:S(2)}, u32[]{:S(2)}) collective-permute-start(bf16[4,80,384]{2,1,0:T(8,128)(2,1)S(1)} %pad_maximum_fusion.r0), channel_id=1, source_target_pairs={{8,0},{12,4},{16,8},{20,12},{24,16},{28,20},{32,24},{36,28},{40,32... | collective-permute-start | bytes 737288 | tf_op jit(solution)/shard_map/ppermute | solution.py:251
  22.4 10.4 %collective-permute-start.5 = (bf16[4,80,384]{2,1,0:T(8,128)(2,1)S(1)}, bf16[4,80,384]{2,1,0:T(8,128)(2,1)S(1)}, u32[]{:S(2)}, u32[]{:S(2)}) collective-permute-start(bf16[4,80,384]{2,1,0:T(8,128)(2,1)S(1)} %pad_maximum_fusion.r0), channel_id=1, source_target_pairs={{4,0},{8,4},{12,8},{16,12},{20,16},{24,20},{28,24},{32,28},{36,32}... | collective-permute-start | bytes 737288 | tf_op jit(solution)/shard_map/ppermute | solution.py:251
  24.3 11.7 %collective-permute-start.4 = (bf16[4,80,384]{2,1,0:T(8,128)(2,1)S(1)}, bf16[4,80,384]{2,1,0:T(8,128)(2,1)S(1)}, u32[]{:S(2)}, u32[]{:S(2)}) collective-permute-start(bf16[4,80,384]{2,1,0:T(8,128)(2,1)S(1)} %pad_maximum_fusion.r0), channel_id=1, source_target_pairs={{0,4},{4,8},{8,12},{12,16},{16,20},{20,24},{24,28},{28,32},{32,36}... | collective-permute-start | bytes 737288 | tf_op jit(solution)/shard_map/ppermute | solution.py:251
  26.7 14.6 %collective-permute-start.3 = (bf16[4,80,384]{2,1,0:T(8,128)(2,1)S(1)}, bf16[4,80,384]{2,1,0:T(8,128)(2,1)S(1)}, u32[]{:S(2)}, u32[]{:S(2)}) collective-permute-start(bf16[4,80,384]{2,1,0:T(8,128)(2,1)S(1)} %pad_maximum_fusion.r0), channel_id=1, source_target_pairs={{0,8},{4,12},{8,16},{12,20},{16,24},{20,28},{24,32},{28,36},{32,40... | collective-permute-start | bytes 737288 | tf_op jit(solution)/shard_map/ppermute | solution.py:251
  32.8 8.6 %copy-start.3 = (bf16[4,80,384]{2,1,0:T(8,128)(2,1)}, bf16[4,80,384]{2,1,0:T(8,128)(2,1)S(1)}, u32[]{:S(2)}) copy-start(bf16[4,80,384]{2,1,0:T(8,128)(2,1)S(1)} %collective-permute-done.6.rp2) | copy-start | bytes 737284
  32.8 8.6 %copy-start.4 = (bf16[4,80,384]{2,1,0:T(8,128)(2,1)}, bf16[4,80,384]{2,1,0:T(8,128)(2,1)S(1)}, u32[]{:S(2)}) copy-start(bf16[4,80,384]{2,1,0:T(8,128)(2,1)S(1)} %collective-permute-done.5.rp1) | copy-start | bytes 737284
  36.1 5.3 %copy-start.5 = (bf16[4,80,384]{2,1,0:T(8,128)(2,1)}, bf16[4,80,384]{2,1,0:T(8,128)(2,1)S(1)}, u32[]{:S(2)}) copy-start(bf16[4,80,384]{2,1,0:T(8,128)(2,1)S(1)} %collective-permute-done.4.rm1) | copy-start | bytes 737284
  41.3 0.7 copy-start.6

commit v2 on v1

v2 whole, which is shorter than its diff:
```python
import math

import jax
import jax.numpy as jnp
import numpy as np
from jax import lax
from jax.experimental import pallas as pl
from jax.experimental.pallas import tpu as pltpu
from jax.sharding import PartitionSpec as P

BF = jnp.bfloat16
F32 = jnp.float32
HEADS, HD, D, CIN, NK = 8, 48, 384, 72, 9
LON, LANES, NSEC, NROW = 360, 384, 4, 3
NLON, NLAT = 1440, 64
WIDE = NSEC * LANES
CP = 80
HR = 64
NEG = -1e30


def lon_table():
    pair = np.arange(24)
    lane = np.arange(7 * LANES)
    lon = ((lane // LANES) % NSEC) * LON + lane % LANES
    angle = 2.0 * math.pi / NLON * lon[None, :] * np.where(pair < 12, pair + 1, 0)[:, None]
    return np.stack([np.cos(angle), np.sin(angle)]).astype(np.float32)


def lat_table():
    pair = np.arange(24)
    row = np.arange(NLAT + 2) - 1
    lat = math.pi / NLAT * (row[:, None] + 0.5) * np.where(pair >= 12, pair - 11, 0)[None, :]
    return np.stack([np.cos(lat), np.sin(lat)], 1).astype(np.float32)


def dot(a, b):
    return jnp.dot(a, b, preferred_element_type=F32)


def make_encoder(own):
    def kernel(odd, fa, fb, fc, wenc, wqkv, gain, tab, kv_out, *rest):
        if own:
            q_out, hid_out, ff, toep, gath, conv, norm = rest
        else:
            ff, toep, gath, conv, norm = rest
        raw = (fa, fb, fc)
        lane = lax.broadcasted_iota(jnp.int32, (CP, 128), 1)
        for row in range(3):
            for u in range(NSEC):
                left = raw[row][(u + 3) % 4, :, 256:384].astype(F32)
                right = raw[row][(u + 1) % 4, :, 0:128].astype(F32)
                first = raw[row][u, :, 0:128].astype(F32)
                last = raw[row][u, :, 256:384].astype(F32)
                first = jnp.where(lane < 8, pltpu.roll(left, 24, 1), first)
                turned = pltpu.roll(right, 104, 1)
                last = jnp.where((lane >= 112) & (lane < 120), turned, last)
                ff[row, u, :, 0:128] = first.astype(BF)
                ff[row, u, :, 128:256] = raw[row][u, :, 128:256]
                ff[row, u, :, 256:384] = last.astype(BF)
        toep[432:512, :] = jnp.zeros((80, NK * 128), BF)
        jp = lax.broadcasted_iota(jnp.int32, (128, 128), 0)
        jj = lax.broadcasted_iota(jnp.int32, (128, 128), 1)
        flip = odd[0] > 0
        for k in range(NK):
            block = fb[k // 8, 72:80, :].astype(F32)[k % 8 : k % 8 + 1]
            for a in range(3):
                tap = jnp.where(
                    flip,
                    block[:, (2 - a) * 128 : (2 - a) * 128 + 128],
                    block[:, a * 128 : a * 128 + 128],
                )
                circ = pltpu.roll(
                    jnp.broadcast_to(tap, (128, 128)), 0, 1, stride=1, stride_axis=0
                )
                main = jnp.where(jj <= jp, circ, 0.0).astype(BF)
                tail = jnp.where(jj > jp, circ, 0.0)[0:16].astype(BF)
                toep[a * 128 : a * 128 + 128, k * 128 : k * 128 + 128] = main
                toep[384 + a * 16 : 400 + a * 16, k * 128 : k * 128 + 128] = tail
        for u in range(NSEC):
            for t in range(3):
                at = (u * 3 + t) * CP
                for a in range(3):
                    gath[at : at + CP, a * 128 : a * 128 + 128] = ff[
                        a, u, :, t * 128 : t * 128 + 128
                    ]
                if t < 2:
                    nxt = [ff[a, u, :, t * 128 + 128 : t * 128 + 256].astype(F32) for a in range(3)]
                    rest_ = jnp.where(
                        lane < 32, pltpu.roll(nxt[1], 16, 1), pltpu.roll(nxt[2], 32, 1)
                    )
                    rest_ = jnp.where(lane < 16, nxt[0], rest_)
                    gath[at : at + CP, 384:512] = rest_.astype(BF)
                else:
                    gath[at : at + CP, 384:512] = jnp.zeros((CP, 128), BF)
        for kk in range(5):
            lo, hi = kk * 256, min(kk * 256 + 256, NK * 128)
            got = dot(gath[...], toep[:, lo:hi]).astype(BF)
            for k in range(2 * kk, min(2 * kk + 2, NK)):
                sub = got[:, (k - 2 * kk) * 128 : (k - 2 * kk) * 128 + 128]
                for t in range(12):
                    conv[k * CP : k * CP + CP, t * 128 : t * 128 + 128] = sub[t * CP : t * CP + CP]
        for n in range(3):
            cols = slice(n * 512, n * 512 + 512)
            pre = dot(wenc[...], conv[:, cols])
            inner = pre * (0.7978845608028654 + 0.035677408136300125 * (pre * pre))
            half = 0.5 * pre
            hid = half + half * jnp.tanh(inner)
            hid = hid.astype(BF).astype(F32)
            scale = lax.rsqrt(jnp.sum(hid * hid, 0, keepdims=True) * (1.0 / D) + 1e-5)
            for i in range(4):
                part = slice(i * 128, i * 128 + 128)
                norm[:, n * 512 + i * 128 : n * 512 + i * 128 + 128] = (
                    hid[:, part] * scale[:, part] * gain[...]
                ).astype(BF)
            if own and n == 0:
                hid_out[...] = jnp.transpose(hid[:, 0:LANES])[0:LON]

        def rotate(x, cols):
            c, s = tab[0, :, cols], tab[1, :, cols]
            x1, x2 = x[0:24], x[24:48]
            return jnp.concatenate([x1 * c - x2 * s, x1 * s + x2 * c], 0)

        sub16 = lax.broadcasted_iota(jnp.int32, (16, LANES), 0)
        lane16 = lax.broadcasted_iota(jnp.int32, (16, LANES), 1)
        if own:
            qt = dot(wqkv[0:D, :], norm[:, 0:LANES])
            zero = jnp.zeros((16, LANES), F32)
            for h in range(HEADS):
                qh = rotate(qt[h * HD : h * HD + HD], slice(0, LANES))
                q_out[h] = jnp.transpose(jnp.concatenate([qh, zero], 0))[0:LON].astype(BF)
        for n in range(3):
            cols = slice(n * 512, n * 512 + 512)
            kv = dot(wqkv[D : 3 * D, :], norm[:, cols])
            for h in range(HEADS):
                kv_out[0, h, 0:HD, cols] = rotate(kv[h * HD : h * HD + HD], cols).astype(BF)
                kv_out[1, h, 0:HD, cols] = kv[D + h * HD : D + h * HD + HD].astype(BF)
        ones = jnp.where(sub16 == 0, 1.0, 0.0).astype(BF)
        for u in range(NSEC):
            mark = (sub16 == u + 1) | ((sub16 == 0) & (lane16 >= LON))
            mark = jnp.where(mark, 1.0, 0.0).astype(BF)
            for h in range(HEADS):
                kv_out[0, h, HD:HR, u * LANES : u * LANES + LANES] = mark
                kv_out[1, h, HD:HR, u * LANES : u * LANES + LANES] = ones

    return kernel


def encode_call(own, odd, rows, wenc, wqkv, gain, tab):
    vm = pl.BlockSpec(memory_space=pltpu.VMEM)
    out_shape = [jax.ShapeDtypeStruct((2, HEADS, HR, WIDE), BF)]
    if own:
        out_shape += [
            jax.ShapeDtypeStruct((HEADS, LON, HR), BF),
            jax.ShapeDtypeStruct((LON, D), F32),
        ]
    return pl.pallas_call(
        make_encoder(own),
        out_shape=out_shape,
        in_specs=[pl.BlockSpec(memory_space=pltpu.SMEM)] + [vm] * 7,
        out_specs=[vm] * len(out_shape),
        scratch_shapes=[
            pltpu.VMEM((3, NSEC, CP, LANES), BF),
            pltpu.VMEM((512, NK * 128), BF),
            pltpu.VMEM((12 * CP, 512), BF),
            pltpu.VMEM((NK * CP, WIDE), BF),
            pltpu.VMEM((D, WIDE), BF),
        ],
        compiler_params=pltpu.CompilerParams(vmem_limit_bytes=24 * 1024 * 1024),
        cost_estimate=pl.CostEstimate(
            flops=5_000_000_000, bytes_accessed=6_000_000, transcendentals=600_000
        ),
        name="encode_own" if own else "encode_outer",
    )(odd, *rows, wenc, wqkv, gain, tab)


QB = 120


def attend_kernel(keep, temper, kv0, kv1, kv2, qs, hid, wout, out, att):
    kvs = (kv0, kv1, kv2)
    lane = lax.broadcasted_iota(jnp.int32, (1, HR), 1)
    bias = []
    for r in range(NROW):
        row = jnp.where(lane == HD, NEG, 0.0)
        for u in range(NSEC):
            off = jnp.where(keep[r * NSEC + u] > 0, 0.0, NEG)
            row = jnp.where(lane == HD + 1 + u, off, row)
        bias.append(row.astype(BF))

    def attend(h2, carry):
        for b in range(LON // QB):
            pieces = []
            for hh in range(2):
                h = h2 * 2 + hh
                q = qs[h, b * QB : b * QB + QB, :]
                s = [dot(q + bias[r], kvs[r][0, h]) for r in range(NROW)]
                peak = jnp.max(jnp.maximum(jnp.maximum(s[0], s[1]), s[2]), 1, keepdims=True)
                acc = jnp.zeros((QB, HR), F32)
                for r in range(NROW):
                    w = jnp.exp2((s[r] - peak) * temper[h]).astype(BF)
                    acc = acc + lax.dot_general(
                        w, kvs[r][1, h], (((1,), (1,)), ((), ())), preferred_element_type=F32
                    )
                pieces.append(acc / acc[:, HD : HD + 1])
            att[h2, b * QB : b * QB + QB, :] = jnp.concatenate(pieces, 1).astype(BF)
        return carry

    lax.fori_loop(0, HEADS // 2, attend, 0)
    mixed = dot(att[0], wout[0:128, :])
    for i in range(1, 4):
        mixed = mixed + dot(att[i], wout[i * 128 : i * 128 + 128, :])
    out[...] = (hid[...] + mixed).astype(BF)


def attend_call(keep, temper, kvs, qs, hid, wout):
    vm = pl.BlockSpec(memory_space=pltpu.VMEM)
    sm = pl.BlockSpec(memory_space=pltpu.SMEM)
    return pl.pallas_call(
        attend_kernel,
        out_shape=jax.ShapeDtypeStruct((LON, D), BF),
        in_specs=[sm, sm] + [vm] * 6,
        out_specs=vm,
        scratch_shapes=[pltpu.VMEM((4, LON, 128), BF)],
        compiler_params=pltpu.CompilerParams(vmem_limit_bytes=32 * 1024 * 1024),
        cost_estimate=pl.CostEstimate(
            flops=14_000_000_000, bytes_accessed=10_000_000, transcendentals=13_000_000
        ),
        name="attend",
    )(keep, temper, *kvs, qs, hid, wout)


def prepare_weights(w_enc, gain, w_qkv, w_out, tau):
    wenc = jnp.pad(jnp.transpose(w_enc, (2, 0, 1)), ((0, 0), (0, 0), (0, CP - CIN)))
    wenc = wenc.reshape(D, NK * CP)
    wout = jnp.pad(w_out.reshape(HEADS, HD, D), ((0, 0), (0, HR - HD), (0, 0)))
    wide_gain = jnp.broadcast_to(gain[:, None], (D, 128))
    temper = tau * (math.log2(math.e) / math.sqrt(HD))
    return wenc, w_qkv.T, wout.reshape(HEADS * HR, D), wide_gain, temper


def prepare_taps(filters, reach):
    f = filters[:, 0]
    offsets = jnp.abs(jnp.arange(17, dtype=jnp.int32) - 8)
    f = jnp.where(offsets[None, None, :] <= reach[0], f, 0.0)
    base = jnp.concatenate([f[:, :, 0:1], jnp.zeros((NK, 3, 111), F32), f[:, :, :0:-1]], -1)
    base = jnp.pad(base.reshape(NK, LANES), ((0, 32 - NK), (0, 0))).astype(BF)
    return base.reshape(4, 8, LANES)


def prepare_field(field):
    return jnp.pad(field[0].T, ((0, 0), (8, LANES - LON - 8)))


def rel_keep(neighbours, s, odd):
    nb = neighbours[0, 0]
    two = jnp.concatenate([nb, nb], 1)
    rel = lax.dynamic_slice(two, (0, s), (NROW, NSEC))
    outer = jnp.where(odd, rel[2], rel[0])
    inner = jnp.where(odd, rel[0], rel[2])
    return jnp.concatenate([rel[1], outer, inner])


def rotary(b, s, outer):
    lon = lax.dynamic_slice(jnp.asarray(lon_table()), (0, 0, s * LANES), (2, 24, WIDE))
    lat = jnp.asarray(lat_table())
    low = lax.broadcasted_iota(jnp.int32, (2, 24, WIDE), 1) < 12
    pick = lambda i: lax.dynamic_index_in_dim(lat, i + 1, 0, keepdims=False)[:, :, None]
    return [jnp.where(low, lon, pick(i)) for i in (b, outer)]


def local(field, filters, reach, w_enc, gain, w_qkv, w_out, tau, neighbours):
    nb, ns = lax.axis_size("band"), lax.axis_size("sector")
    b, s = lax.axis_index("band"), lax.axis_index("sector")
    odd = b % 2
    outer = b + 2 * odd - 1
    mine = prepare_field(field)
    got = [lax.ppermute(mine, "sector", [((i + u) % ns, i) for i in range(ns)]) for u in (1, 2, 3)]
    row = jnp.concatenate([jnp.stack([mine] + got), prepare_taps(filters, reach)], 1)
    side = [(i + 1 if i % 2 else i - 1, i) for i in range(nb)]
    side = [pair for pair in side if 0 <= pair[0] < nb]
    twin = [(i ^ 1, i) for i in range(nb)]
    near = lax.ppermute(row, "band", side)
    chip = lax.ppermute(row, "band", twin)
    far = lax.ppermute(chip, "band", side)
    wenc, wqkv, wout, wide_gain, temper = prepare_weights(w_enc, gain, w_qkv, w_out, tau)
    tabs = rotary(b, s, outer)
    flag = odd.astype(jnp.int32).reshape(1)
    kv_own, qs, hid = encode_call(True, flag, [near, row, chip], wenc, wqkv, wide_gain, tabs[0])
    kv_chip = lax.ppermute(kv_own, "band", twin)
    (kv_outer,) = encode_call(False, flag, [far, near, row], wenc, wqkv, wide_gain, tabs[1])
    keep = rel_keep(neighbours, s, odd == 1)
    return attend_call(keep, temper, [kv_own, kv_outer, kv_chip], qs, hid, wout)[None]


def solution(mesh):
    return jax.shard_map(
        local,
        mesh=mesh,
        in_specs=(
            P("band", "sector", None),
            P(None, "band", None, None),
            P("band"),
            P(),
            P(),
            P(),
            P(),
            P(),
            P("band", "sector", None, None),
        ),
        out_specs=P("band", "sector", None),
        check_vma=False,
    )
```

time: 81 us -> 76.7 us (0.947)
  the two profiles are of different devices: /device:TPU:32 before, /device:TPU:31 now
where the time goes in v2:
time: 76.7 us; the launch traced here: 76.4 us
  Pallas kernels  35 us (46%)
  waiting for transfers between devices  17.8 us (23%)
  starting transfers between devices  15.4 us (20%)
  local copies, waits for them, and re-layouts  6.21 us (8%)
  other arithmetic  1.12 us (1%)
  between operations  0.87 us (1%)
    pallas_call x1, Pallas kernels, attend_call(): pl.pallas_call(attend_kernel, out_shape=jax.ShapeDtypeStruct((LON, D), BF...  24.4 us
    pallas_call x2, Pallas kernels, encode_call(): pl.pallas_call(make_encoder(own), out_shape=out_shape, in_specs=[pl.Block...  10.7 us
    ppermute x1, waiting for transfers between devices, local(): near = lax.ppermute(row, 'band', side)  9.46 us
    ppermute x3, starting transfers between devices, local(): lax.ppermute(mine, 'sector', [((i + u) % ns, i) for i in range(ns)])  9.36 us
    ppermute x1, waiting for transfers between devices, local(): far = lax.ppermute(chip, 'band', side)  8.31 us
    ppermute x1, starting transfers between devices, local(): far = lax.ppermute(chip, 'band', side)  2.3 us
    ppermute x1, starting transfers between devices, local(): near = lax.ppermute(row, 'band', side)  2.12 us
    unnamed x18, local copies, waits for them, and re-layouts  1.72 us
  transfers between devices with their start and end apart: 7, of which 2 were waited for; matrix products, arithmetic and copies ran while one was open for 7% of the time, Pallas kernels for 6%

profile of v2, /device:TPU:31, one launch (start us, length us, event | category | flops | bytes accessed | tf_op | source)
XLA Modules:
  0.0 76.4 jit_solution(16988383767834583856)
XLA Ops:
  0.0 0.0 copy-start.3
  0.0 0.0 copy-start.2
  0.0 0.0 copy-start.4
  0.0 1.0 %pad_bitcast_fusion.1 = (bf16[1,72,384]{2,1,0:T(8,128)(2,1)S(1)}, bf16[72,384]{1,0:T(8,128)(2,1)S(1)}) fusion(bf16[72,360]{1,0:T(8,128)(2,1)} %bitcast.46), kind=kLoop, calls=%fused_computation.21 | loop fusion | bytes 162432 | tf_op jit(solution)/shard_map/stack | solution.py:279
  1.0 7.0 %collective-permute-start.1 = (bf16[72,384]{1,0:T(8,128)(2,1)S(1)}, bf16[72,384]{1,0:T(8,128)(2,1)S(1)}, u32[]{:S(2)}, u32[]{:S(2)}) collective-permute-start(bf16[72,384]{1,0:T(8,128)(2,1)S(1)} %get-tuple-element.16), channel_id=1, source_target_pairs={{2,0},{3,1},{0,2},{1,3},{6,4},{7,5},{4,6},{5,7},{10,8},{11,9},{8,1... | collective-permute-start | bytes 165896 | tf_op jit(solution)/shard_map/ppermute | solution.py:278
  8.0 0.0 collective-permute-start
  8.0 2.4 %collective-permute-start.2 = (bf16[72,384]{1,0:T(8,128)(2,1)S(1)}, bf16[72,384]{1,0:T(8,128)(2,1)S(1)}, u32[]{:S(2)}, u32[]{:S(2)}) collective-permute-start(bf16[72,384]{1,0:T(8,128)(2,1)S(1)} %get-tuple-element.16), channel_id=1, source_target_pairs={{3,0},{0,1},{1,2},{2,3},{7,4},{4,5},{5,6},{6,7},{11,8},{8,9},{9,10... | collective-permute-start | bytes 165896 | tf_op jit(solution)/shard_map/ppermute | solution.py:278
  11.1 0.7 bitcast_select_fusion
  11.8 0.1 slice.24
  11.9 0.1 rev.3
  12.0 0.1 pad.27.clone
  12.0 0.1 pad_maximum_fusion.1
  12.2 0.7 dynamic-slice_bitcast_fusion
  12.9 1.1 %pad.19 = bf16[384,9,80]{0,2,1:T(8,128)(2,1)S(1)} pad(bf16[384,9,72]{0,2,1:T(8,128)(2,1)} %bitcast.42, bf16[]{:T(256)} %constant.53.clone.1), padding=0_0x0_0x0_8 | pad | bytes 1050626 | tf_op jit(solution)/shard_map/jit(_pad)/pad | solution.py:234
  14.0 0.3 copy.15.wenc
  14.2 0.0 copy-done.2
  14.2 0.9 %copy.14 = bf16[384,1152]{0,1:T(8,128)(2,1)S(1)} copy(bf16[384,1152]{1,0:T(8,128)(2,1)S(1)} %copy-done.2) | data formatting | bytes 1769472 | tf_op args[5]
  15.1 0.0 collective-permute-done.1
  15.1 0.0 collective-permute-done
  15.1 0.0 collective-permute-done.2
  15.2 1.6 %collective-permute-start.4 = (bf16[4,80,384]{2,1,0:T(8,128)(2,1)S(1)}, bf16[4,80,384]{2,1,0:T(8,128)(2,1)S(1)}, u32[]{:S(2)}, u32[]{:S(2)}) collective-permute-start(bf16[4,80,384]{2,1,0:T(8,128)(2,1)S(1)} %pad_maximum_fusion.fb.fc), channel_id=1, source_target_pairs={{4,0},{0,4},{12,8},{8,12},{20,16},{16,20},{28,24},{24,28},{36,32},... | collective-permute-start | bytes 737288 | tf_op jit(solution)/shard_map/ppermute | solution.py:284
  16.8 2.1 %collective-permute-start.3 = (bf16[4,80,384]{2,1,0:T(8,128)(2,1)S(1)}, bf16[4,80,384]{2,1,0:T(8,128)(2,1)S(1)}, u32[]{:S(2)}, u32[]{:S(2)}) collective-permute-start(bf16[4,80,384]{2,1,0:T(8,128)(2,1)S(1)} %pad_maximum_fusion.fb.fc), channel_id=1, source_target_pairs={{8,4},{4,8},{16,12},{12,16},{24,20},{20,24},{32,28},{28,32},{40,36... | collective-permute-start | bytes 737288 | tf_op jit(solution)/shard_map/ppermute | solution.py:283
  18.9 0.0 copy-done.3
  18.9 0.1 dynamic-slice_select_fusion
  19.0 0.0 collective-permute-done.4.fc
  19.1 9.5 %collective-permute-done.3.fa.fb = bf16[4,80,384]{2,1,0:T(8,128)(2,1)S(1)} collective-permute-done((bf16[4,80,384]{2,1,0:T(8,128)(2,1)S(1)}, bf16[4,80,384]{2,1,0:T(8,128)(2,1)S(1)}, u32[]{:S(2)}, u32[]{:S(2)}) %collective-permute-start.3) | collective-permute-done | bytes 245792 | tf_op jit(solution)/shard_map/ppermute | solution.py:283
  28.5 0.0 copy-done.4
  28.5 0.1 broadcast_in_dim.47.gain
  28.6 0.0 copy-start.5
  28.6 0.0 copy-start.6
  28.6 6.3 %encode_own.1 = (bf16[2,8,64,1536]{3,2,1,0:T(8,128)(2,1)}, bf16[8,360,64]{2,1,0:T(8,128)(2,1)S(1)}, f32[360,384]{1,0:T(8,128)S(1)}) custom-call(s32[1]{0:T(128)} %bitcast.3.odd, bf16[4,80,384]{2,1,0:T(8,128)(2,1)S(1)} %collective-permute-done.3.fa.fb, bf16[4,80,384]{2,1,0:T(8,128)(2,1)S(1)} %pad_maximum_fusion.fb.fc, ...), custom_call_target="tpu_custom_call" | custom-call | flops 5000000000 | bytes 6000000 | tf_op jit(solution)/shard_map/encode_own/pallas_call | solution.py:157
  34.9 0.0 copy-start
  34.9 0.8 %copy-done = f32[360,384]{1,0:T(8,128)} copy-done((f32[360,384]{1,0:T(8,128)}, f32[360,384]{1,0:T(8,128)S(1)}, u32[]{:S(2)}) %copy-start) | copy-done | bytes 552984
  35.7 0.0 collective-permute-start.6
  35.7 0.0 copy-done.5
  35.7 0.1 pad_add_fusion
  35.8 0.1 constant_dynamic-slice_fusion
  35.9 2.3 %collective-permute-start.5 = (bf16[4,80,384]{2,1,0:T(8,128)(2,1)S(1)}, bf16[4,80,384]{2,1,0:T(8,128)(2,1)S(1)}, u32[]{:S(2)}, u32[]{:S(2)}) collective-permute-start(bf16[4,80,384]{2,1,0:T(8,128)(2,1)S(1)} %collective-permute-done.4.fc), channel_id=1, source_target_pairs={{8,4},{4,8},{16,12},{12,16},{24,20},{20,24},{32,28},{28,32},{40,36... | collective-permute-start | bytes 737288 | tf_op jit(solution)/shard_map/ppermute | solution.py:285
  38.2 0.1 pad_add_fusion.1.keep
  38.3 1.0 %pad.20 = bf16[8,64,384]{2,1,0:T(8,128)(2,1)S(1)} pad(bf16[8,48,384]{2,1,0:T(8,128)(2,1)} %bitcast.43, bf16[]{:T(256)} %constant.53.clone.1), padding=0_0x0_16x0_0 | pad | bytes 688130 | tf_op jit(solution)/shard_map/jit(_pad)/pad | solution.py:236
  39.3 0.0 copy-done.6
  39.3 8.3 %collective-permute-done.5.fa = bf16[4,80,384]{2,1,0:T(8,128)(2,1)S(1)} collective-permute-done((bf16[4,80,384]{2,1,0:T(8,128)(2,1)S(1)}, bf16[4,80,384]{2,1,0:T(8,128)(2,1)S(1)}, u32[]{:S(2)}, u32[]{:S(2)}) %collective-permute-start.5) | collective-permute-done | bytes 245792 | tf_op jit(solution)/shard_map/ppermute | solution.py:285
  47.6 0.0 copy-start.1
  47.6 4.4 %encode_outer.1.kv1 = bf16[2,8,64,1536]{3,2,1,0:T(8,128)(2,1)S(1)} custom-call(s32[1]{0:T(128)} %bitcast.3.odd, bf16[4,80,384]{2,1,0:T(8,128)(2,1)S(1)} %collective-permute-done.5.fa, bf16[4,80,384]{2,1,0:T(8,128)(2,1)S(1)} %collective-permute-done.3.fa.fb, bf16[4,80,384]{2,1,0:T(8,128)(2,1)S(1)} %pad_maximum_fusion.fb.fc, bf16[384,720]{1,0:T(8,128)(2,1)S(1)} %copy.15.wenc, ...), custom_call_target="tpu_custom_call" | custom-call | flops 5000000000 | bytes 6000000 | tf_op jit(solution)/shard_map/encode_outer/pallas_call | solution.py:157
  52.0 0.0 collective-permute-done.6.kv2
  52.0 0.0 copy-done.1
  52.0 24.4 %attend.1 = bf16[360,384]{1,0:T(8,128)(2,1)} custom-call(s32[12]{0:T(128)S(1)} %pad_add_fusion.1.keep, f32[8]{0:T(128)S(1)} %broadcast_multiply_fusion.temper, bf16[2,8,64,1536]{3,2,1,0:T(8,128)(2,1)} %get-tuple-element.8.kv0, bf16[2,8,64,1536]{3,2,1,0:T(8,128)(2,1)S(1)} %encode_outer.1.kv1, bf16[2,8,64,1536]{3,2,1,0:T(8,128)(2,1)} %collective-permute-done.6.kv2, ...), custom_call_target="tpu_custom_call" | custom-call | flops 14000000000 | bytes 10000000 | tf_op jit(solution)/shard_map/attend/pallas_call | solution.py:219
  (10 shorter events, 0.1 us)
Async XLA Ops:
  0.0 18.9 %copy-start.3 = (f32[2,24,2688]{2,1,0:T(8,128)S(1)}, f32[2,24,2688]{2,1,0:T(8,128)}, u32[]{:S(2)}) copy-start(f32[2,24,2688]{2,1,0:T(8,128)} %constant.61.clone) | copy-start | bytes 1548292
  0.0 14.2 %copy-start.2 = (bf16[384,1152]{1,0:T(8,128)(2,1)S(1)}, bf16[384,1152]{1,0:T(8,128)(2,1)}, u32[]{:S(2)}) copy-start(bf16[384,1152]{1,0:T(8,128)(2,1)} %param.16) | copy-start | bytes 2654212
  0.0 28.5 %copy-start.4 = (f32[384]{0:T(512)S(1)}, f32[384]{0:T(512)}, u32[]{:S(2)}) copy-start(f32[384]{0:T(512)} %param.15) | copy-start | bytes 4612
  1.0 14.1 %collective-permute-start.1 = (bf16[72,384]{1,0:T(8,128)(2,1)S(1)}, bf16[72,384]{1,0:T(8,128)(2,1)S(1)}, u32[]{:S(2)}, u32[]{:S(2)}) collective-permute-start(bf16[72,384]{1,0:T(8,128)(2,1)S(1)} %get-tuple-element.16), channel_id=1, source_target_pairs={{2,0},{3,1},{0,2},{1,3},{6,4},{7,5},{4,6},{5,7},{10,8},{11,9},{8,1... | collective-permute-start | bytes 165896 | tf_op jit(solution)/shard_map/ppermute | solution.py:278
  8.0 7.1 %collective-permute-start = (bf16[72,384]{1,0:T(8,128)(2,1)S(1)}, bf16[72,384]{1,0:T(8,128)(2,1)S(1)}, u32[]{:S(2)}, u32[]{:S(2)}) collective-permute-start(bf16[72,384]{1,0:T(8,128)(2,1)S(1)} %get-tuple-element.16), channel_id=1, source_target_pairs={{1,0},{2,1},{3,2},{0,3},{5,4},{6,5},{7,6},{4,7},{9,8},{10,9},{11,1... | collective-permute-start | bytes 165896 | tf_op jit(solution)/shard_map/ppermute | solution.py:278
  8.0 7.1 %collective-permute-start.2 = (bf16[72,384]{1,0:T(8,128)(2,1)S(1)}, bf16[72,384]{1,0:T(8,128)(2,1)S(1)}, u32[]{:S(2)}, u32[]{:S(2)}) collective-permute-start(bf16[72,384]{1,0:T(8,128)(2,1)S(1)} %get-tuple-element.16), channel_id=1, source_target_pairs={{3,0},{0,1},{1,2},{2,3},{7,4},{4,5},{5,6},{6,7},{11,8},{8,9},{9,10... | collective-permute-start | bytes 165896 | tf_op jit(solution)/shard_map/ppermute | solution.py:278
  15.2 3.9 %collective-permute-start.4 = (bf16[4,80,384]{2,1,0:T(8,128)(2,1)S(1)}, bf16[4,80,384]{2,1,0:T(8,128)(2,1)S(1)}, u32[]{:S(2)}, u32[]{:S(2)}) collective-permute-start(bf16[4,80,384]{2,1,0:T(8,128)(2,1)S(1)} %pad_maximum_fusion.fb.fc), channel_id=1, source_target_pairs={{4,0},{0,4},{12,8},{8,12},{20,16},{16,20},{28,24},{24,28},{36,32},... | collective-permute-start | bytes 737288 | tf_op jit(solution)/shard_map/ppermute | solution.py:284
  16.8 11.7 %collective-permute-start.3 = (bf16[4,80,384]{2,1,0:T(8,128)(2,1)S(1)}, bf16[4,80,384]{2,1,0:T(8,128)(2,1)S(1)}, u32[]{:S(2)}, u32[]{:S(2)}) collective-permute-start(bf16[4,80,384]{2,1,0:T(8,128)(2,1)S(1)} %pad_maximum_fusion.fb.fc), channel_id=1, source_target_pairs={{8,4},{4,8},{16,12},{12,16},{24,20},{20,24},{32,28},{28,32},{40,36... | collective-permute-start | bytes 737288 | tf_op jit(solution)/shard_map/ppermute | solution.py:283
  28.6 7.1 %copy-start.5 = (s32[1,1,3,4]{3,1,2,0:T(1,128)S(1)}, s32[1,1,3,4]{3,1,2,0:T(1,128)}, u32[]{:S(2)}) copy-start(s32[1,1,3,4]{3,1,2,0:T(1,128)} %param.19) | copy-start | bytes 148
  28.6 10.7 %copy-start.6 = (f32[8]{0:T(128)S(1)}, f32[8]{0:T(128)}, u32[]{:S(2)}) copy-start(f32[8]{0:T(128)} %param.18) | copy-start | bytes 100
  34.9 0.8 %copy-start = (f32[360,384]{1,0:T(8,128)}, f32[360,384]{1,0:T(8,128)S(1)}, u32[]{:S(2)}) copy-start(f32[360,384]{1,0:T(8,128)S(1)} %get-tuple-element.10.hid) | copy-start | bytes 1658884
  35.7 16.3 %collective-permute-start.6 = (bf16[2,8,64,1536]{3,2,1,0:T(8,128)(2,1)}, bf16[2,8,64,1536]{3,2,1,0:T(8,128)(2,1)}, u32[]{:S(2)}, u32[]{:S(2)}) collective-permute-start(bf16[2,8,64,1536]{3,2,1,0:T(8,128)(2,1)} %get-tuple-element.8.kv0), channel_id=1, source_target_pairs={{4,0},{0,4},{12,8},{8,12},{20,16},{16,20},{28,24},{24,28},{36,32},... | collective-permute-start | bytes 9437192 | tf_op jit(solution)/shard_map/ppermute | solution.py:290
  35.9 11.7 %collective-permute-start.5 = (bf16[4,80,384]{2,1,0:T(8,128)(2,1)S(1)}, bf16[4,80,384]{2,1,0:T(8,128)(2,1)S(1)}, u32[]{:S(2)}, u32[]{:S(2)}) collective-permute-start(bf16[4,80,384]{2,1,0:T(8,128)(2,1)S(1)} %collective-permute-done.4.fc), channel_id=1, source_target_pairs={{8,4},{4,8},{16,12},{12,16},{24,20},{20,24},{32,28},{28,32},{40,36... | collective-permute-start | bytes 737288 | tf_op jit(solution)/shard_map/ppermute | solution.py:285
  47.6 4.4 %copy-start.1 = (f32[360,384]{1,0:T(8,128)S(1)}, f32[360,384]{1,0:T(8,128)}, u32[]{:S(2)}) copy-start(f32[360,384]{1,0:T(8,128)} %copy-done) | copy-start | bytes 1658884
